TPU v7x, 32 devices: a whole 2x2x4 slice. The times are simulated.
32 devices in a mesh: dp: 4 (over z), seq: 8 (over y, x, core).
Axes of the slice: x: 2, y: 2, z: 4, core: 2. Of those that a mesh axis runs over, the one named last changes fastest.
Arguments:
- patches: bfloat16 [6144, 1280], P(('dp', 'seq')), may hold values from -6 to 6
- query_key_value: bfloat16 [6144, 3840], P(('dp', 'seq')), may hold values from -100 to 100
- counts: int32 [32, 4], P(('dp', 'seq')), may hold values from 4 to 48, as said below
- owner_index: int32 [1536, 1], P(('dp', 'seq')), may hold values from 0 to 7; in each aligned block of 48 rows (0 to 47, 48 to 95, ...) at most 6 rows name the same one
- out_weight: bfloat16 [1280, 1280], P(None, 'dp'), may hold values from -0.15625 to 0.15625
- ln_gain: float32 [1280], replicated, may hold values from 0.25 to 1.75
- ln_bias: float32 [1280], replicated, may hold values from -3 to 3
Outputs:
- image_tokens: bfloat16 [1536, 5120], P(('dp', 'seq'))
Inputs may be any that keep to these rules, and one draw needn't show every extreme that they name: Every count is a multiple of 4, each device's counts sum to at most 192, and some device's counts sum to exactly 192. `owner_index`: among the merge groups of one device, at most 6 name the same owner.
All inputs are finite; a program needn't handle non-finite values.
Results may differ from a plain program's by a relative error of at most 0.0029.
Values may be sent and summed in bfloat16 or wider, within the bound.
A program may use at most 64 MiB of HBM per device.

v0:
```python
import jax
import jax.numpy as jnp
from jax import lax
from jax.sharding import PartitionSpec as P

HEADS = 16
IMGS = 4


def segment_rows(count_row, row_count):
    image_ends = jnp.cumsum(count_row)
    row_ids = jnp.arange(row_count, dtype=jnp.int32)
    return jnp.sum((row_ids[:, None] >= image_ends[None, :]).astype(jnp.int32), axis=1)


def attend(packed, segment_ids, model_width):
    row_count = packed.shape[0]
    head_size = model_width // HEADS
    queries = packed[:, :model_width].reshape(row_count, HEADS, head_size)
    keys_all = packed[:, model_width : 2 * model_width].reshape(row_count, HEADS, head_size)
    values_all = packed[:, 2 * model_width :].reshape(row_count, HEADS, head_size)
    scores = jnp.einsum(
        "qhd,khd->hqk", queries, keys_all, preferred_element_type=jnp.float32
    ) * head_size ** (-0.5)
    same_image = segment_ids[:, None] == segment_ids[None, :]
    scores = jnp.where(same_image[None, :, :], scores, -1e30)
    top_score = jnp.max(scores, axis=2, keepdims=True)
    expo = jnp.exp(scores - top_score)
    attn_weights = (expo / jnp.sum(expo, axis=2, keepdims=True)).astype(jnp.bfloat16)
    context = jnp.einsum(
        "hqk,khd->qhd", attn_weights, values_all, preferred_element_type=jnp.float32
    )
    return context.reshape(row_count, model_width).astype(jnp.bfloat16)


def merge_and_place(hidden, segment_ids, owners, ln_gain, ln_bias, owner_count, capacity):
    row_count, model_width = hidden.shape
    row_mean = jnp.mean(hidden, axis=1, keepdims=True)
    centered = hidden - row_mean
    row_var = jnp.mean(centered * centered, axis=1, keepdims=True)
    normed = (centered * lax.rsqrt(row_var + 1e-06) * ln_gain[None, :] + ln_bias[None, :]).astype(
        jnp.bfloat16
    )
    merged = normed.reshape(row_count // 4, 4 * model_width)
    live_group = segment_ids.reshape(row_count // 4, 4)[:, 0] < IMGS
    group_ids = jnp.arange(row_count // 4, dtype=jnp.int32)
    earlier = (
        (owners[None, :] == owners[:, None])
        & (group_ids[None, :] < group_ids[:, None])
        & live_group[None, :]
    )
    slot_index = jnp.sum(earlier.astype(jnp.int32), axis=1)
    target = owners * capacity + slot_index
    slot_ids = jnp.arange(owner_count * capacity, dtype=jnp.int32)
    onehot_map = ((slot_ids[:, None] == target[None, :]) & live_group[None, :]).astype(jnp.bfloat16)
    return jnp.dot(onehot_map, merged, preferred_element_type=jnp.float32).astype(jnp.bfloat16)


def body(patches, query_key_value, counts, owner_index, out_weight, ln_gain, ln_bias):
    row_count, model_width = patches.shape
    owner_count = lax.axis_size("seq")
    group_count = row_count // 4
    capacity = max(2, (group_count + owner_count - 1) // owner_count)
    segment_ids = segment_rows(counts[0], row_count)
    context = attend(query_key_value, segment_ids, model_width)
    slice_rows = model_width // owner_count
    own_slice = lax.dynamic_slice_in_dim(
        out_weight, lax.axis_index("seq") * slice_rows, slice_rows, 0
    )
    weight_slab = lax.all_gather(own_slice, "dp", axis=1, tiled=True)
    projected = jnp.dot(
        context,
        lax.all_gather(weight_slab, "seq", axis=0, tiled=True),
        preferred_element_type=jnp.float32,
    )
    hidden = patches.astype(jnp.float32) + projected
    outgoing = merge_and_place(
        hidden, segment_ids, owner_index[:, 0], ln_gain, ln_bias, owner_count, capacity
    )
    outgoing = outgoing.reshape(owner_count, capacity, 4 * model_width)
    received = lax.all_to_all(outgoing, "seq", split_axis=0, concat_axis=0, tiled=True)
    return received.reshape(owner_count * capacity, 4 * model_width)


def solution(mesh):
    placed = (
        P(("dp", "seq"), None),
        P(("dp", "seq"), None),
        P(("dp", "seq"), None),
        P(("dp", "seq"), None),
        P(None, "dp"),
        P(),
        P(),
    )
    return jax.shard_map(
        body, mesh=mesh, in_specs=placed, out_specs=P(("dp", "seq"), None), check_vma=False
    )
```

profile of v0, /device:TPU:0, one launch (start us, length us, event | category | flops | bytes accessed | tf_op | source)
XLA Modules:
  0.0 86.8 jit_solution(10084298187133097372)
XLA Ops:
  6.5 0.0 copy-start
  6.5 0.0 all-gather.3.cloned.1.call-start
  6.5 1.1 %copy-done = bf16[1280,320]{0,1:T(8,128)(2,1)S(1)} copy-done((bf16[1280,320]{0,1:T(8,128)(2,1)S(1)}, bf16[1280,320]{0,1:T(8,128)(2,1)}, u32[]{:S(2)}) %copy-start) | copy-done | bytes 819224
  7.7 0.1 constant_dynamic-slice_fusion
  7.8 0.1 copy.38
  7.9 17.1 %all-gather = bf16[4,320,160]{1,2,0:T(8,128)(2,1)S(1)} all-gather(bf16[1,320,160]{1,2,0:T(8,128)(2,1)S(1)} %bitcast.29), channel_id=1, replica_groups=mesh['dp'=4,'seq'=8] {'dp'}, dimensions={0}, use_global_device_ids=true | all-gather | bytes 512000 | tf_op jit(solution)/shard_map/all_gather | solution.py:70
  25.0 0.3 copy.36
  25.3 0.0 copy-start.6
  25.3 1.1 %reshape.116 = bf16[1280,160]{0,1:T(8,128)(2,1)} reshape(bf16[4,320,160]{1,0,2:T(4,128)(2,1)S(1)} %copy.36) | data formatting | bytes 819200
  26.5 0.0 all-gather.3.cloned.1.call-update
  26.5 0.0 copy-start.5
  26.5 1.4 %fusion.18 = (bf16[192,1280]{1,0:T(8,128)(2,1)S(1)}, bf16[192,1280]{1,0:T(8,128)(2,1)S(1)}, bf16[192,1280]{1,0:T(8,128)(2,1)S(1)}) fusion(bf16[192,3840]{1,0:T(8,128)(2,1)} %param.8), kind=kLoop, calls=%fused_computation.34 | loop fusion | bytes 2949120 | tf_op jit(solution)/shard_map/slice | solution.py:20
  27.9 0.2 copy.31
  28.2 0.2 copy.32
  28.4 0.0 copy-done.6
  28.4 0.2 reduce-window.8
  28.6 1.1 %copy.33 = bf16[192,1280]{0,1:T(8,128)(2,1)} copy(bf16[192,1280]{1,0:T(8,128)(2,1)S(1)} %get-tuple-element.7) | data formatting | bytes 983040 | tf_op jit(solution)/shard_map/slice | solution.py:21
  29.7 0.1 convert_reduce_fusion.1
  29.8 0.1 reshape.108
  29.9 0.1 fusion.13
  30.0 0.0 copy-done.5
  30.0 0.2 convert_reduce_fusion
  30.2 0.1 broadcast_compare_fusion
  30.3 0.0 copy-start.1
  30.3 3.0 %fusion.19 = (f32[16,192]{1,0:T(8,128)S(1)}, f32[16,192,192]{1,2,0:T(8,128)}) fusion(pred[192,192]{0,1:T(8,128)(4,1)S(1)} %broadcast_compare_fusion, bf16[192,16,80]{0,2,1:T(8,128)(2,1)S(1)} %bitcast.26, bf16[192,16,80]{0,2,1:T(8,128)(2,1)S(1)} %bitcast.27), kind=kOutput, calls=%fused_computation.35 | convolution fusion | flops 96731328 | bytes 3391488 | tf_op jit(solution)/shard_map/sub | solution.py:28
  33.3 0.0 copy-done.1
  33.3 0.0 copy-start.2
  33.3 2.4 %fusion.6 = bf16[16,192,80]{1,2,0:T(8,128)(2,1)S(1)} fusion(bf16[192,16,80]{0,2,1:T(8,128)(2,1)S(1)} %bitcast.28, f32[16,192,192]{1,2,0:T(8,128)} %get-tuple-element.9, f32[16,192]{1,0:T(8,128)S(1)} %get-tuple-element.8), kind=kOutput, calls=%fused_computation.11 | convolution fusion | flops 95797248 | bytes 3354624 | tf_op jit(solution)/shard_map/hqk,khd->qhd/dot_general | solution.py:30
  35.7 25.4 %all-gather.3.cloned.1.call-done = bf16[1280,1280]{1,0:T(8,128)(2,1)} async-done(((bf16[160,1280]{1,0:T(8,128)(2,1)}), bf16[1280,1280]{1,0:T(8,128)(2,1)}) %all-gather.3.cloned.1.call-update) | async-done | bytes 3276816 | tf_op jit(solution)/shard_map/all_gather | solution.py:73
  61.1 0.0 copy-done.2
  61.1 0.0 copy-start.3
  61.1 0.0 copy-start.4
  61.1 2.9 %fusion.20 = (f32[192]{0:T(256)S(1)}, f32[192,1280]{1,0:T(8,128)S(1)}) fusion(bf16[192,1280]{0,1:T(8,128)(2,1)S(1)} %bitcast.25, bf16[1280,1280]{1,0:T(8,128)(2,1)} %all-gather.3.cloned.1.call-done, bf16[192,1280]{1,0:T(8,128)(2,1)S(1)} %copy-done.2), kind=kOutput, calls=%fused_computation.36 | convolution fusion | flops 629882688 | bytes 5243648 | tf_op jit(solution)/shard_map/dot_general | solution.py:71
  64.0 0.2 multiply_reduce_fusion
  64.3 0.0 copy-done.3
  64.3 0.0 copy-done.4
  64.3 0.2 add_convert_fusion
  64.6 0.3 reshape.112
  64.9 0.3 convolution_convert_fusion
  65.2 0.2 reshape.113
  65.3 13.7 %all_to_all.5 = bf16[8,6,5120]{2,1,0:T(8,128)(2,1)S(1)} all-to-all(bf16[8,6,5120]{2,1,0:T(8,128)(2,1)S(1)} %reshape.113), channel_id=1, replica_groups=mesh['dp'=4,'seq'=8] {'seq'}, dimensions={0} | all-to-all | bytes 983040 | tf_op jit(solution)/shard_map/all_to_all | solution.py:81
  79.0 1.0 %reshape.114 = bf16[48,5120]{1,0:T(8,128)(2,1)} reshape(bf16[8,6,5120]{2,1,0:T(8,128)(2,1)S(1)} %all_to_all.5) | data formatting | bytes 983040 | tf_op jit(solution)/shard_map/reshape | solution.py:82
  (3 shorter events, 0.0 us)
Async XLA Ops:
  6.5 1.1 %copy-start = (bf16[1280,320]{0,1:T(8,128)(2,1)S(1)}, bf16[1280,320]{0,1:T(8,128)(2,1)}, u32[]{:S(2)}) copy-start(bf16[1280,320]{0,1:T(8,128)(2,1)} %param.11) | copy-start | bytes 2457604
  6.5 54.6 %all-gather.3.cloned.1.call-start = ((), (), s32[]{:S(2)}) async-start(), calls=%async_computation.1 | async-start | bytes 3686400 | tf_op jit(solution)/shard_map/all_gather | solution.py:73
  25.3 3.1 %copy-start.6 = (s32[1,4]{1,0:T(1,128)S(1)}, s32[1,4]{1,0:T(1,128)}, u32[]{:S(2)}) copy-start(s32[1,4]{1,0:T(1,128)} %param.9) | copy-start | bytes 52
  26.5 3.5 %copy-start.5 = (s32[48,1]{0,1:T(1,128)S(1)}, s32[48,1]{0,1:T(1,128)}, u32[]{:S(2)}) copy-start(s32[48,1]{0,1:T(1,128)} %param.10) | copy-start | bytes 580
  30.3 3.0 %copy-start.1 = (bf16[192,1280]{0,1:T(8,128)(2,1)S(1)}, bf16[192,1280]{0,1:T(8,128)(2,1)}, u32[]{:S(2)}) copy-start(bf16[192,1280]{0,1:T(8,128)(2,1)} %copy.33) | copy-start | bytes 1474564
  33.3 27.8 %copy-start.2 = (bf16[192,1280]{1,0:T(8,128)(2,1)S(1)}, bf16[192,1280]{1,0:T(8,128)(2,1)}, u32[]{:S(2)}) copy-start(bf16[192,1280]{1,0:T(8,128)(2,1)} %param.7) | copy-start | bytes 1474564
  61.1 3.2 %copy-start.3 = (f32[1280]{0:T(1024)S(1)}, f32[1280]{0:T(1024)}, u32[]{:S(2)}) copy-start(f32[1280]{0:T(1024)} %param.13) | copy-start | bytes 15364
  61.1 3.2 %copy-start.4 = (f32[1280]{0:T(1024)S(1)}, f32[1280]{0:T(1024)}, u32[]{:S(2)}) copy-start(f32[1280]{0:T(1024)} %param.12) | copy-start | bytes 15364
Sparse Core Ops, SparseCore 0:
  26.6 34.4 all-gather.2
where the time goes:
time: 87 us; the launch traced here: 86.8 us
  blocking collectives  30.8 us (35%)
  waiting for transfers between devices  25.4 us (29%)
  between operations  13.5 us (16%)
  matrix products  8.57 us (10%)
  local copies, waits for them, and re-layouts  7.35 us (8%)
  other arithmetic  1.17 us (1%)
    all_gather x1, waiting for transfers between devices, body(): lax.all_gather(weight_slab, 'seq', axis=0, tiled=True)  25.4 us
    all_gather x1, blocking collectives, body(): weight_slab = lax.all_gather(own_slice, 'dp', axis=1, tiled=True)  17.1 us
    all_to_all x1, blocking collectives, body(): lax.all_to_all(outgoing, 'seq', split_axis=0, concat_axis=0, tiled=True)  13.7 us
    sub x1, matrix products, attend(): expo = jnp.exp(scores - top_score)  2.97 us
    dot_general x1, matrix products, body(): jnp.dot(context, lax.all_gather(weight_slab, 'seq', axis=0, tiled=True),...  2.89 us
    unnamed x16, local copies, waits for them, and re-layouts  2.45 us
    dot_general x1, matrix products, attend(): jnp.einsum('hqk,khd->qhd', attn_weights, values_all, preferred_element_ty...  2.44 us
  transfers between devices with their start and end apart: 1, of which 1 were waited for; matrix products, arithmetic and copies ran while one was open for 11% of the time, Pallas kernels for 0%

commit v1 on v0

--- a/solution.py
+++ b/solution.py
@@ -5,6 +5,19 @@
 
 HEADS = 16
 IMGS = 4
+
+
+def collect(x, axis, dim):
+    ways = lax.axis_size(axis)
+    up = [(d, (d + 1) % ways) for d in range(ways)]
+    down = [(d, (d - 1) % ways) for d in range(ways)]
+    earlier, later = ([x], [x])
+    for _ in range(ways // 2):
+        earlier.append(lax.ppermute(earlier[-1], axis, up))
+    for _ in range((ways - 1) // 2):
+        later.append(lax.ppermute(later[-1], axis, down))
+    line = jnp.concatenate([*earlier[::-1], *later[1:]], axis=dim)
+    return jnp.roll(line, (lax.axis_index(axis) - ways // 2) * x.shape[dim], axis=dim)
 
 
 def segment_rows(count_row, row_count):
@@ -67,7 +80,7 @@
     own_slice = lax.dynamic_slice_in_dim(
         out_weight, lax.axis_index("seq") * slice_rows, slice_rows, 0
     )
-    weight_slab = lax.all_gather(own_slice, "dp", axis=1, tiled=True)
+    weight_slab = collect(own_slice, "dp", 1)
     projected = jnp.dot(
         context,
         lax.all_gather(weight_slab, "seq", axis=0, tiled=True),

time: 87 us -> 83.5 us (0.960)
  blocking collectives: 30.8 us -> 13.7 us
  waiting for transfers between devices: 25.4 us -> 34.6 us
  starting transfers between devices: 0.01 us -> 5.2 us
    all_gather x1 -> x0, blocking collectives: 17.1 us -> none  [body(): weight_slab = lax.all_gather(own_slice, 'dp', axis=1, tiled=True)]
    ppermute x0 -> x3, waiting for transfers between devices: none -> 10.8 us  [the longest x2 9.57 us: collect(): earlier.append(lax.ppermute(earlier[-1], axis, up))]
    ppermute x0 -> x3, starting transfers between devices: none -> 5.2 us  [the longest x2 3.11 us: collect(): earlier.append(lax.ppermute(earlier[-1], axis, up))]
    all_gather x1, waiting for transfers between devices: 25.4 us -> 23.8 us  [body(): lax.all_gather(weight_slab, 'seq', axis=0, tiled=True)]
    unnamed x16 -> x13, local copies, waits for them, and re-layouts: 2.45 us -> 1.29 us
    dynamic_slice x0 -> x1, local copies, waits for them, and re-layouts: none -> 0.94 us  [collect(): jnp.roll(line, (lax.axis_index(axis) - ways // 2) * x.shape[dim], axis=dim)]
  transfers between devices with their start and end apart: 1 -> 4, of which waited for: 1 -> 4; matrix products, arithmetic and copies ran while one was open for 11% -> 10% of each run, Pallas kernels for 0% -> 0%
where the time goes in v1:
time: 83.5 us; the launch traced here: 83.2 us
  waiting for transfers between devices  34.6 us (41%)
  blocking collectives  13.7 us (16%)
  between operations  13.5 us (16%)
  matrix products  8.57 us (10%)
  local copies, waits for them, and re-layouts  6.52 us (8%)
  starting transfers between devices  5.2 us (6%)
  other arithmetic  1.17 us (1%)
    all_gather x1, waiting for transfers between devices, body(): lax.all_gather(weight_slab, 'seq', axis=0, tiled=True)  23.8 us
    all_to_all x1, blocking collectives, body(): lax.all_to_all(outgoing, 'seq', split_axis=0, concat_axis=0, tiled=True)  13.7 us
    ppermute x2, waiting for transfers between devices, collect(): earlier.append(lax.ppermute(earlier[-1], axis, up))  9.57 us
    ppermute x2, starting transfers between devices, collect(): earlier.append(lax.ppermute(earlier[-1], axis, up))  3.11 us
    sub x1, matrix products, attend(): expo = jnp.exp(scores - top_score)  2.95 us
    dot_general x1, matrix products, body(): jnp.dot(context, lax.all_gather(weight_slab, 'seq', axis=0, tiled=True),...  2.88 us
    dot_general x1, matrix products, attend(): jnp.einsum('hqk,khd->qhd', attn_weights, values_all, preferred_element_ty...  2.48 us
    ppermute x1, starting transfers between devices, collect(): later.append(lax.ppermute(later[-1], axis, down))  2.09 us
  transfers between devices with their start and end apart: 4, of which 4 were waited for; matrix products, arithmetic and copies ran while one was open for 10% of the time, Pallas kernels for 0%

profile of v1, /device:TPU:0, one launch (start us, length us, event | category | flops | bytes accessed | tf_op | source)
XLA Modules:
  0.0 83.2 jit_solution(1255777648605047926)
XLA Ops:
  6.5 0.0 copy-start
  6.5 0.0 all-gather.2.cloned.1.call-start
  6.5 1.1 %copy-done = bf16[1280,320]{0,1:T(8,128)(2,1)S(1)} copy-done((bf16[1280,320]{0,1:T(8,128)(2,1)S(1)}, bf16[1280,320]{0,1:T(8,128)(2,1)}, u32[]{:S(2)}) %copy-start) | copy-done | bytes 819224
  7.7 0.1 constant_dynamic-slice_fusion.1
  7.8 0.1 copy.31
  7.9 3.1 %collective-permute-start = (bf16[160,320]{1,0:T(8,128)(2,1)S(1)}, bf16[160,320]{1,0:T(8,128)(2,1)S(1)}, u32[]{:S(2)}, u32[]{:S(2)}) collective-permute-start(bf16[160,320]{1,0:T(8,128)(2,1)S(1)} %copy.31), channel_id=1, source_target_pairs={{0,8},{8,16},{16,24},{24,0},{1,9},{9,17},{17,25},{25,1},{2,10},{10... | collective-permute-start | bytes 307208 | tf_op jit(solution)/shard_map/ppermute | solution.py:16
  11.0 2.1 %collective-permute-start.2 = (bf16[160,320]{1,0:T(8,128)(2,1)S(1)}, bf16[160,320]{1,0:T(8,128)(2,1)S(1)}, u32[]{:S(2)}, u32[]{:S(2)}) collective-permute-start(bf16[160,320]{1,0:T(8,128)(2,1)S(1)} %copy.31), channel_id=1, source_target_pairs={{0,24},{8,0},{16,8},{24,16},{1,25},{9,1},{17,9},{25,17},{2,26},{10... | collective-permute-start | bytes 307208 | tf_op jit(solution)/shard_map/ppermute | solution.py:18
  13.1 4.1 %collective-permute-done = bf16[160,320]{1,0:T(8,128)(2,1)S(1)} collective-permute-done((bf16[160,320]{1,0:T(8,128)(2,1)S(1)}, bf16[160,320]{1,0:T(8,128)(2,1)S(1)}, u32[]{:S(2)}, u32[]{:S(2)}) %collective-permute-start) | collective-permute-done | bytes 102432 | tf_op jit(solution)/shard_map/ppermute | solution.py:16
  17.2 0.0 collective-permute-start.1
  17.2 0.0 copy-start.5
  17.2 1.2 %collective-permute-done.2 = bf16[160,320]{1,0:T(8,128)(2,1)S(1)} collective-permute-done((bf16[160,320]{1,0:T(8,128)(2,1)S(1)}, bf16[160,320]{1,0:T(8,128)(2,1)S(1)}, u32[]{:S(2)}, u32[]{:S(2)}) %collective-permute-start.2) | collective-permute-done | bytes 102432 | tf_op jit(solution)/shard_map/ppermute | solution.py:18
  18.5 5.5 %collective-permute-done.1 = bf16[160,320]{1,0:T(8,128)(2,1)S(1)} collective-permute-done((bf16[160,320]{1,0:T(8,128)(2,1)S(1)}, bf16[160,320]{1,0:T(8,128)(2,1)S(1)}, u32[]{:S(2)}, u32[]{:S(2)}) %collective-permute-start.1) | collective-permute-done | bytes 102432 | tf_op jit(solution)/shard_map/ppermute | solution.py:16
  23.9 0.5 concatenate.6
  24.4 0.9 %constant_dynamic-slice_fusion = bf16[160,1280]{1,0:T(8,128)(2,1)} fusion(bf16[160,2560]{1,0:T(8,128)(2,1)S(1)} %concatenate.6, s32[]{:T(128)S(6)} %select_n.23), kind=kLoop, calls=%fused_computation.30 | loop fusion | bytes 819204 | tf_op jit(solution)/shard_map/jit(_roll_dynamic)/dynamic_slice | solution.py:20
  25.4 0.0 all-gather.2.cloned.1.call-update
  25.4 0.0 copy-start.4
  25.4 1.4 %fusion.18 = (bf16[192,1280]{1,0:T(8,128)(2,1)S(1)}, bf16[192,1280]{1,0:T(8,128)(2,1)S(1)}, bf16[192,1280]{1,0:T(8,128)(2,1)S(1)}) fusion(bf16[192,3840]{1,0:T(8,128)(2,1)} %param.8), kind=kLoop, calls=%fused_computation.35 | loop fusion | bytes 2949120 | tf_op jit(solution)/shard_map/slice | solution.py:33
  26.8 0.2 copy.27
  27.1 0.0 copy-done.5
  27.1 0.2 reduce-window.8
  27.3 0.2 copy.25
  27.5 0.2 copy.26
  27.7 0.1 convert_reduce_fusion.1
  27.8 0.1 reshape.108
  27.9 0.1 fusion.13
  28.1 0.0 copy-done.4
  28.1 0.2 convert_reduce_fusion
  28.3 0.1 broadcast_compare_fusion
  28.4 2.9 %fusion.19 = (f32[16,192]{1,0:T(8,128)S(1)}, f32[16,192,192]{1,2,0:T(8,128)}) fusion(pred[192,192]{0,1:T(8,128)(4,1)S(1)} %broadcast_compare_fusion, bf16[192,16,80]{0,2,1:T(8,128)(2,1)S(1)} %bitcast.20, bf16[192,16,80]{0,2,1:T(8,128)(2,1)S(1)} %bitcast.21), kind=kOutput, calls=%fused_computation.36 | convolution fusion | flops 96731328 | bytes 3391488 | tf_op jit(solution)/shard_map/sub | solution.py:41
  31.3 0.0 copy-start.1
  31.3 2.5 %fusion.6 = bf16[16,192,80]{1,2,0:T(8,128)(2,1)S(1)} fusion(bf16[192,16,80]{0,2,1:T(8,128)(2,1)S(1)} %bitcast.19, f32[16,192,192]{1,2,0:T(8,128)} %get-tuple-element.9, f32[16,192]{1,0:T(8,128)S(1)} %get-tuple-element.8), kind=kOutput, calls=%fused_computation.11 | convolution fusion | flops 95797248 | bytes 3354624 | tf_op jit(solution)/shard_map/hqk,khd->qhd/dot_general | solution.py:43
  33.8 23.8 %all-gather.2.cloned.1.call-done = bf16[1280,1280]{1,0:T(8,128)(2,1)} async-done(((bf16[160,1280]{1,0:T(8,128)(2,1)}), bf16[1280,1280]{1,0:T(8,128)(2,1)}) %all-gather.2.cloned.1.call-update) | async-done | bytes 3276816 | tf_op jit(solution)/shard_map/all_gather | solution.py:86
  57.6 0.0 copy-done.1
  57.6 0.0 copy-start.2
  57.6 0.0 copy-start.3
  57.6 2.9 %fusion.20 = (f32[192]{0:T(256)S(1)}, f32[192,1280]{1,0:T(8,128)S(1)}) fusion(bf16[192,1280]{0,1:T(8,128)(2,1)S(1)} %bitcast.18, bf16[1280,1280]{1,0:T(8,128)(2,1)} %all-gather.2.cloned.1.call-done, bf16[192,1280]{1,0:T(8,128)(2,1)S(1)} %copy-done.1), kind=kOutput, calls=%fused_computation.37 | convolution fusion | flops 629882688 | bytes 5243648 | tf_op jit(solution)/shard_map/dot_general | solution.py:84
  60.5 0.2 multiply_reduce_fusion
  60.7 0.0 copy-done.2
  60.7 0.0 copy-done.3
  60.8 0.2 add_convert_fusion
  61.0 0.3 reshape.112
  61.3 0.3 convolution_convert_fusion
  61.6 0.2 reshape.113
  61.8 13.7 %all_to_all.5 = bf16[8,6,5120]{2,1,0:T(8,128)(2,1)S(1)} all-to-all(bf16[8,6,5120]{2,1,0:T(8,128)(2,1)S(1)} %reshape.113), channel_id=1, replica_groups=mesh['dp'=4,'seq'=8] {'seq'}, dimensions={0} | all-to-all | bytes 983040 | tf_op jit(solution)/shard_map/all_to_all | solution.py:94
  75.4 1.0 %reshape.114 = bf16[48,5120]{1,0:T(8,128)(2,1)} reshape(bf16[8,6,5120]{2,1,0:T(8,128)(2,1)S(1)} %all_to_all.5) | data formatting | bytes 983040 | tf_op jit(solution)/shard_map/reshape | solution.py:95
  (3 shorter events, 0.0 us)
Async XLA Ops:
  6.5 1.1 %copy-start = (bf16[1280,320]{0,1:T(8,128)(2,1)S(1)}, bf16[1280,320]{0,1:T(8,128)(2,1)}, u32[]{:S(2)}) copy-start(bf16[1280,320]{0,1:T(8,128)(2,1)} %param.11) | copy-start | bytes 2457604
  6.5 51.0 %all-gather.2.cloned.1.call-start = ((), (), s32[]{:S(2)}) async-start(), calls=%async_computation.1 | async-start | bytes 3686400 | tf_op jit(solution)/shard_map/all_gather | solution.py:86
  7.9 9.3 %collective-permute-start = (bf16[160,320]{1,0:T(8,128)(2,1)S(1)}, bf16[160,320]{1,0:T(8,128)(2,1)S(1)}, u32[]{:S(2)}, u32[]{:S(2)}) collective-permute-start(bf16[160,320]{1,0:T(8,128)(2,1)S(1)} %copy.31), channel_id=1, source_target_pairs={{0,8},{8,16},{16,24},{24,0},{1,9},{9,17},{17,25},{25,1},{2,10},{10... | collective-permute-start | bytes 307208 | tf_op jit(solution)/shard_map/ppermute | solution.py:16
  11.0 7.4 %collective-permute-start.2 = (bf16[160,320]{1,0:T(8,128)(2,1)S(1)}, bf16[160,320]{1,0:T(8,128)(2,1)S(1)}, u32[]{:S(2)}, u32[]{:S(2)}) collective-permute-start(bf16[160,320]{1,0:T(8,128)(2,1)S(1)} %copy.31), channel_id=1, source_target_pairs={{0,24},{8,0},{16,8},{24,16},{1,25},{9,1},{17,9},{25,17},{2,26},{10... | collective-permute-start | bytes 307208 | tf_op jit(solution)/shard_map/ppermute | solution.py:18
  17.2 6.7 %collective-permute-start.1 = (bf16[160,320]{1,0:T(8,128)(2,1)S(1)}, bf16[160,320]{1,0:T(8,128)(2,1)S(1)}, u32[]{:S(2)}, u32[]{:S(2)}) collective-permute-start(bf16[160,320]{1,0:T(8,128)(2,1)S(1)} %collective-permute-done), channel_id=1, source_target_pairs={{0,8},{8,16},{16,24},{24,0},{1,9},{9,17},{17,25},{25,1},{2,10},{10... | collective-permute-start | bytes 307208 | tf_op jit(solution)/shard_map/ppermute | solution.py:16
  17.2 9.8 %copy-start.5 = (s32[1,4]{1,0:T(1,128)S(1)}, s32[1,4]{1,0:T(1,128)}, u32[]{:S(2)}) copy-start(s32[1,4]{1,0:T(1,128)} %param.9) | copy-start | bytes 52
  25.4 2.7 %copy-start.4 = (s32[48,1]{0,1:T(1,128)S(1)}, s32[48,1]{0,1:T(1,128)}, u32[]{:S(2)}) copy-start(s32[48,1]{0,1:T(1,128)} %param.10) | copy-start | bytes 580
  31.3 26.3 %copy-start.1 = (bf16[192,1280]{1,0:T(8,128)(2,1)S(1)}, bf16[192,1280]{1,0:T(8,128)(2,1)}, u32[]{:S(2)}) copy-start(bf16[192,1280]{1,0:T(8,128)(2,1)} %param.7) | copy-start | bytes 1474564
  57.6 3.2 %copy-start.2 = (f32[1280]{0:T(1024)S(1)}, f32[1280]{0:T(1024)}, u32[]{:S(2)}) copy-start(f32[1280]{0:T(1024)} %param.13) | copy-start | bytes 15364
  57.6 3.2 %copy-start.3 = (f32[1280]{0:T(1024)S(1)}, f32[1280]{0:T(1024)}, u32[]{:S(2)}) copy-start(f32[1280]{0:T(1024)} %param.12) | copy-start | bytes 15364
Sparse Core Ops, SparseCore 0:
  25.5 32.0 all-gather.1
